TPU v7x, 32 devices: a whole 2x2x4 slice. The times are simulated.
32 devices in a mesh: ctx: 8 (over y, x, core), exp: 4 (over z).
Axes of the slice: x: 2, y: 2, z: 4, core: 2. Of those that a mesh axis runs over, the one named last changes fastest.
Arguments:
- tokens: bfloat16 [4096, 2048], P(('ctx', 'exp')), may hold values from -6 to 6
- cotangent: bfloat16 [4096, 2048], P(('ctx', 'exp')), may hold values from -6 to 6
- expert_ids: int32 [4096, 1], P(('ctx', 'exp')), may hold values from 0 to 3; in each aligned block of 128 rows (0 to 127, 128 to 255, ...) at most 48 rows name the same one
- route_weights: float32 [4096, 1], P(('ctx', 'exp')), may hold values from 0.1 to 1
- w_gate: bfloat16 [4, 2048, 768], P('exp', 'ctx'), may hold values from -0.125 to 0.125
- w_up: bfloat16 [4, 2048, 768], P('exp', 'ctx'), may hold values from -0.125 to 0.125
- w_down: bfloat16 [4, 768, 2048], P('exp', None, 'ctx'), may hold values from -0.21875 to 0.21875
Outputs:
- token_grads: bfloat16 [4096, 2048], P(('ctx', 'exp'))
- route_grads: float32 [4096, 1], P(('ctx', 'exp'))
- gate_grads: bfloat16 [4, 2048, 768], P('exp', 'ctx')
- up_grads: bfloat16 [4, 2048, 768], P('exp', 'ctx')
- down_grads: bfloat16 [4, 768, 2048], P('exp', None, 'ctx')
Inputs may be any that keep to these rules, and one draw needn't show every extreme that they name: `expert_ids`: among the 128 routes of one device's tokens no expert is named more than 48 times, a bound that some block reaches; the routes of one token name different experts.
All inputs are finite; a program needn't handle non-finite values.
Results may differ from a plain program's by a relative error of at most 0.018.
Values may be sent and summed in bfloat16 or wider, within the bound.
A program may use at most 64 MiB of HBM per device.

v0:
```python
import jax
import jax.numpy as jnp
from jax import lax
from jax.sharding import PartitionSpec as P


def slot_table(route_ids, expert_count, capacity):
    labels = jnp.arange(expert_count, dtype=jnp.int32)
    onehot = (route_ids[..., :, None] == labels).astype(jnp.int32)
    position = jnp.sum((jnp.cumsum(onehot, axis=-2) - 1) * onehot, axis=-1)
    target = route_ids * capacity + position
    places = jnp.arange(expert_count * capacity, dtype=jnp.int32)
    return (target[..., None, :] == places[:, None]).astype(jnp.bfloat16)


def forward_hidden(totals, units):
    gate_pre = totals[:, :units]
    up_pre = totals[:, units:]
    gate_sig = jax.nn.sigmoid(gate_pre)
    return (gate_pre * gate_sig * up_pre).astype(jnp.bfloat16)


def backward_grads(totals, back_sum, units):
    gate_pre = totals[:, :units]
    up_pre = totals[:, units:]
    gate_sig = jax.nn.sigmoid(gate_pre)
    d_up = (back_sum * gate_pre * gate_sig).astype(jnp.bfloat16)
    d_gate = (back_sum * up_pre * gate_sig * (1.0 + gate_pre * (1.0 - gate_sig))).astype(
        jnp.bfloat16
    )
    return jnp.concatenate([d_gate, d_up], axis=1)


def body(tokens, cotangent, expert_ids, route_weights, w_gate, w_up, w_down):
    ctx_size = lax.axis_size("ctx")
    exp_size = lax.axis_size("exp")
    tok_count, model_width = tokens.shape
    route_count = expert_ids.shape[1]
    slot_count = tok_count * route_count
    expert_count = w_gate.shape[0] * exp_size
    capacity = max(2, (3 * slot_count + 2 * expert_count - 1) // (2 * expert_count))
    col_count = model_width // ctx_size
    units = w_gate.shape[2]
    row_count = ctx_size * exp_size * capacity
    own_rows = row_count // ctx_size
    all_ids = lax.all_gather(expert_ids, "ctx", axis=0, tiled=True)
    tables = slot_table(all_ids.reshape(ctx_size, slot_count), expert_count, capacity)
    token_slots = jnp.repeat(tokens, route_count, axis=0)
    scaled = (
        route_weights * jnp.repeat(cotangent, route_count, axis=0).astype(jnp.float32)
    ).astype(jnp.bfloat16)
    own_table = lax.dynamic_index_in_dim(tables, lax.axis_index("ctx"), 0, keepdims=False)
    send_x = jnp.dot(own_table, token_slots, preferred_element_type=jnp.float32).astype(
        jnp.bfloat16
    )
    send_y = jnp.dot(own_table, scaled, preferred_element_type=jnp.float32).astype(jnp.bfloat16)
    send_x = send_x.reshape(expert_count, capacity, model_width)
    send_y = send_y.reshape(expert_count, capacity, model_width)
    group_x, group_y = (
        lax.all_to_all(send_x, "exp", split_axis=0, concat_axis=0, tiled=True),
        lax.all_to_all(send_y, "exp", split_axis=0, concat_axis=0, tiled=True),
    )
    slot_x, slot_y = (
        lax.all_to_all(group_x, "ctx", split_axis=2, concat_axis=0, tiled=True),
        lax.all_to_all(group_y, "ctx", split_axis=2, concat_axis=0, tiled=True),
    )
    slot_x = slot_x.reshape(row_count, col_count)
    slot_y = slot_y.reshape(row_count, col_count)
    gate_weight = w_gate[0]
    up_weight = w_up[0]
    down_weight = w_down[0]
    both_weights = jnp.concatenate([gate_weight, up_weight], axis=1)

    def fold_grad(segment):
        gate_acc = lax.dot_general(
            slot_x, segment[:, :units], (((0,), (0,)), ((), ())), preferred_element_type=jnp.float32
        )
        up_acc = lax.dot_general(
            slot_x, segment[:, units:], (((0,), (0,)), ((), ())), preferred_element_type=jnp.float32
        )
        grad_rows = lax.dot_general(
            segment, both_weights, (((1,), (1,)), ((), ())), preferred_element_type=jnp.float32
        )
        return (gate_acc, up_acc, grad_rows)

    row_x, row_y = (
        lax.all_to_all(slot_x, "ctx", split_axis=0, concat_axis=1, tiled=True),
        lax.all_to_all(slot_y, "ctx", split_axis=0, concat_axis=1, tiled=True),
    )
    full_gate, full_up, full_down = (
        lax.all_gather(gate_weight, "ctx", axis=0, tiled=True),
        lax.all_gather(up_weight, "ctx", axis=0, tiled=True),
        lax.all_gather(down_weight, "ctx", axis=1, tiled=True),
    )
    full_both = jnp.concatenate([full_gate, full_up], axis=1).reshape(
        ctx_size, col_count, 2 * units
    )
    gate_blocks = jnp.einsum(
        "rcd,cdf->crf",
        row_x.reshape(own_rows, ctx_size, col_count),
        full_both,
        preferred_element_type=jnp.float32,
    ).astype(jnp.bfloat16)
    totals_own = jnp.sum(gate_blocks.astype(jnp.float32), axis=0)
    hidden_own = forward_hidden(totals_own, units)
    back_blocks = jnp.einsum(
        "rcd,fcd->crf",
        row_y.reshape(own_rows, ctx_size, col_count),
        full_down.reshape(units, ctx_size, col_count),
        preferred_element_type=jnp.float32,
    ).astype(jnp.bfloat16)
    back_own = jnp.sum(back_blocks.astype(jnp.float32), axis=0)
    grads_own = backward_grads(totals_own, back_own, units)
    segment = (
        lax.all_gather(hidden_own, "ctx", axis=0, tiled=True),
        lax.all_gather(grads_own, "ctx", axis=0, tiled=True),
    )
    fold_segment = segment[0]
    outputs = jnp.dot(fold_segment, down_weight, preferred_element_type=jnp.float32)
    inner_rows = jnp.sum(slot_y.astype(jnp.float32) * outputs, axis=1)
    inner_all = inner_rows
    down_acc = lax.dot_general(
        fold_segment, slot_y, (((0,), (0,)), ((), ())), preferred_element_type=jnp.float32
    )
    down_state = (down_acc, inner_all)
    grad_state = fold_grad(segment[1])
    down_acc = down_state[0]
    inner_all = down_state[1]
    gate_acc = grad_state[0]
    up_acc = grad_state[1]
    back_rows = grad_state[2]
    back_slots = back_rows.astype(jnp.bfloat16).reshape(ctx_size, exp_size, capacity, col_count)
    inner_slots = inner_all.reshape(ctx_size, exp_size, capacity)
    home_back = lax.all_to_all(back_slots, "exp", split_axis=1, concat_axis=1, tiled=True)
    home_inner = lax.all_to_all(inner_slots, "exp", split_axis=1, concat_axis=1, tiled=True)
    merged = jnp.einsum(
        "cks,ckd->csd",
        tables,
        home_back.reshape(ctx_size, expert_count * capacity, col_count),
        preferred_element_type=jnp.float32,
    )
    merged = jnp.sum(merged.reshape(ctx_size, tok_count, route_count, col_count), axis=2).astype(
        jnp.bfloat16
    )
    grads_home = lax.all_to_all(merged, "ctx", split_axis=0, concat_axis=2, tiled=True)
    token_grads = grads_home.reshape(tok_count, model_width)
    inner_home = jnp.einsum(
        "cks,ck->cs",
        tables.astype(jnp.float32),
        home_inner.reshape(ctx_size, expert_count * capacity),
        precision=lax.Precision.HIGHEST,
    )
    route_sums = lax.psum_scatter(inner_home, "ctx", scatter_dimension=0, tiled=True).reshape(
        tok_count, route_count
    )
    route_grads = route_sums / route_weights
    gate_grads = gate_acc.astype(jnp.bfloat16)[None]
    up_grads = up_acc.astype(jnp.bfloat16)[None]
    down_grads = down_acc.astype(jnp.bfloat16)[None]
    return (token_grads, route_grads, gate_grads, up_grads, down_grads)


def solution(mesh):
    return jax.shard_map(
        body,
        mesh=mesh,
        in_specs=(
            P(("ctx", "exp"), None),
            P(("ctx", "exp"), None),
            P(("ctx", "exp"), None),
            P(("ctx", "exp"), None),
            P("exp", "ctx", None),
            P("exp", "ctx", None),
            P("exp", None, "ctx"),
        ),
        out_specs=(
            P(("ctx", "exp"), None),
            P(("ctx", "exp"), None),
            P("exp", "ctx", None),
            P("exp", "ctx", None),
            P("exp", None, "ctx"),
        ),
        check_vma=False,
    )
```

profile of v0, /device:TPU:0, one launch (start us, length us, event | category | flops | bytes accessed | tf_op | source)
XLA Modules:
  0.0 269.7 jit_solution(1433237262053152039)
XLA Ops:
  7.2 2.0 copy.87
  10.7 10.3 %all_gather.18 = s32[1024,1]{0,1:T(1,128)S(1)} all-gather(s32[128,1]{0,1:T(1,128)} %param.9), channel_id=1, replica_groups=mesh['ctx'=8,'exp'=4] {'ctx'}, dimensions={0}, use_global_device_ids=true | all-gather | bytes 4608 | tf_op jit(solution)/shard_map/all_gather | solution.py:46
  21.1 2.5 select_reduce_fusion
  23.8 2.4 convolution_convert_fusion.2
  26.2 4.9 %all-to-all-start = ((bf16[4,48,2048]{2,1,0:T(8,128)(2,1)}), bf16[4,48,2048]{2,1,0:T(8,128)(2,1)S(1)}, u32[]{:S(2)}, u32[]{:S(2)}) async-start(bf16[4,48,2048]{2,1,0:T(8,128)(2,1)} %bitcast.3), calls=%async_computation | async-start | bytes 1572864 | tf_op jit(solution)/shard_map/all_to_all | solution.py:61
  31.1 1.3 convolution_convert_fusion.1
  32.4 19.3 %all-to-all-done = bf16[4,48,2048]{2,1,0:T(8,128)(2,1)S(1)} async-done(((bf16[4,48,2048]{2,1,0:T(8,128)(2,1)}), bf16[4,48,2048]{2,1,0:T(8,128)(2,1)S(1)}, u32[]{:S(2)}, u32[]{:S(2)}) %all-to-all-start) | async-done | bytes 786464 | tf_op jit(solution)/shard_map/all_to_all | solution.py:61
  51.7 0.9 copy-done.1
  52.6 3.5 %all-to-all-start.3 = ((bf16[4,48,2048]{2,1,0:T(8,128)(2,1)}), bf16[4,48,2048]{2,1,0:T(8,128)(2,1)S(1)}, u32[]{:S(2)}, u32[]{:S(2)}) async-start(bf16[4,48,2048]{2,1,0:T(8,128)(2,1)} %bitcast.10), calls=%async_computation.3 | async-start | bytes 1572864 | tf_op jit(solution)/shard_map/all_to_all | solution.py:60
  56.1 2.9 %copy.84 = bf16[4,48,2048]{1,0,2:T(4,128)(2,1)S(1)} copy(bf16[4,48,2048]{2,1,0:T(8,128)(2,1)} %copy-done.1) | data formatting | bytes 1572864 | tf_op jit(solution)/shard_map/all_to_all | solution.py:61
  59.0 4.0 %reshape.98 = bf16[8,2,24576]{2,1,0:T(2,128)(2,1)} reshape(bf16[2048,4,48]{2,1,0:T(4,128)(2,1)S(1)} %bitcast.76) | data formatting | bytes 1572864
  63.0 12.9 %all-to-all-done.3 = bf16[4,48,2048]{2,1,0:T(8,128)(2,1)S(1)} async-done(((bf16[4,48,2048]{2,1,0:T(8,128)(2,1)}), bf16[4,48,2048]{2,1,0:T(8,128)(2,1)S(1)}, u32[]{:S(2)}, u32[]{:S(2)}) %all-to-all-start.3) | async-done | bytes 786464 | tf_op jit(solution)/shard_map/all_to_all | solution.py:60
  75.8 4.2 %all-to-all-start.1 = ((bf16[8,2,24576]{2,1,0:T(2,128)(2,1)}), bf16[8,2,24576]{2,1,0:T(2,128)(2,1)}, u32[]{:S(2)}, u32[]{:S(2)}) async-start(bf16[8,2,24576]{2,1,0:T(2,128)(2,1)} %reshape.98), calls=%async_computation.1 | async-start | bytes 1572864 | tf_op jit(solution)/shard_map/all_to_all | solution.py:65
  80.1 1.4 copy.89
  81.5 4.0 %reshape.100 = bf16[8,2,24576]{2,1,0:T(2,128)(2,1)} reshape(bf16[2048,4,48]{2,1,0:T(4,128)(2,1)S(1)} %bitcast.77) | data formatting | bytes 1572864
  85.4 7.3 %all-to-all-done.1 = bf16[8,2,24576]{2,1,0:T(2,128)(2,1)} async-done(((bf16[8,2,24576]{2,1,0:T(2,128)(2,1)}), bf16[8,2,24576]{2,1,0:T(2,128)(2,1)}, u32[]{:S(2)}, u32[]{:S(2)}) %all-to-all-start.1) | async-done | bytes 786464 | tf_op jit(solution)/shard_map/all_to_all | solution.py:65
  92.7 3.5 %all-to-all-start.4 = ((bf16[8,2,24576]{2,1,0:T(2,128)(2,1)}), bf16[8,2,24576]{2,1,0:T(2,128)(2,1)S(1)}, u32[]{:S(2)}, u32[]{:S(2)}) async-start(bf16[8,2,24576]{2,1,0:T(2,128)(2,1)} %reshape.100), calls=%async_computation.4 | async-start | bytes 1572864 | tf_op jit(solution)/shard_map/all_to_all | solution.py:64
  96.3 5.7 %reshape.99 = bf16[2048,4,48]{2,1,0:T(4,128)(2,1)S(1)} reshape(bf16[8,2,24576]{2,1,0:T(2,128)(2,1)} %all-to-all-done.1) | data formatting | bytes 1572864
  102.0 2.2 copy.103
  104.1 8.9 %all-to-all-done.4 = bf16[8,2,24576]{2,1,0:T(2,128)(2,1)S(1)} async-done(((bf16[8,2,24576]{2,1,0:T(2,128)(2,1)}), bf16[8,2,24576]{2,1,0:T(2,128)(2,1)S(1)}, u32[]{:S(2)}, u32[]{:S(2)}) %all-to-all-start.4) | async-done | bytes 786464 | tf_op jit(solution)/shard_map/all_to_all | solution.py:64
  113.0 4.4 %all-to-all-start.2 = ((bf16[8,192,256]{2,1,0:T(8,128)(2,1)}), bf16[8,192,256]{2,1,0:T(8,128)(2,1)}, u32[]{:S(2)}, u32[]{:S(2)}) async-start(bf16[8,192,256]{2,1,0:T(8,128)(2,1)} %bitcast.7), calls=%async_computation.2 | async-start | bytes 1572864 | tf_op jit(solution)/shard_map/all_to_all | solution.py:88
  117.4 2.1 reshape.101
  119.5 2.1 copy.90
  121.7 8.2 %all-to-all-done.2 = bf16[8,192,256]{2,1,0:T(8,128)(2,1)} async-done(((bf16[8,192,256]{2,1,0:T(8,128)(2,1)}), bf16[8,192,256]{2,1,0:T(8,128)(2,1)}, u32[]{:S(2)}, u32[]{:S(2)}) %all-to-all-start.2) | async-done | bytes 786464 | tf_op jit(solution)/shard_map/all_to_all | solution.py:88
  129.9 3.5 %all-to-all-start.5 = ((bf16[8,192,256]{2,1,0:T(8,128)(2,1)}), bf16[8,192,256]{2,1,0:T(8,128)(2,1)S(1)}, u32[]{:S(2)}, u32[]{:S(2)}) async-start(bf16[8,192,256]{2,1,0:T(8,128)(2,1)} %bitcast.13), calls=%async_computation.5 | async-start | bytes 1572864 | tf_op jit(solution)/shard_map/all_to_all | solution.py:87
  133.5 3.0 %convert_reduce_fusion.1 = f32[192,768]{1,0:T(8,128)S(1)} fusion(bf16[768,8,256]{0,2,1:T(8,128)(2,1)} %bitcast.95, bf16[8,192,256]{2,1,0:T(8,128)(2,1)} %all-to-all-done.2), kind=kOutput, calls=%fused_computation.2 | convolution fusion | flops 607371264 | bytes 4521984 | tf_op jit(solution)/shard_map/rcd,fcd->crf/dot_general | solution.py:106
  136.5 6.0 %pad_maximum_fusion = bf16[2048,1536]{1,0:T(8,128)(2,1)} fusion(bf16[2048,768]{1,0:T(8,128)(2,1)} %bitcast.83, bf16[2048,768]{1,0:T(8,128)(2,1)} %bitcast.82), kind=kLoop, calls=%fused_computation.1 | loop fusion | flops 12582912 | bytes 12582912 | tf_op jit(solution)/shard_map/concatenate | solution.py:95
  142.5 3.5 %all-to-all-done.5 = bf16[8,192,256]{2,1,0:T(8,128)(2,1)S(1)} async-done(((bf16[8,192,256]{2,1,0:T(8,128)(2,1)}), bf16[8,192,256]{2,1,0:T(8,128)(2,1)S(1)}, u32[]{:S(2)}, u32[]{:S(2)}) %all-to-all-start.5) | async-done | bytes 786464 | tf_op jit(solution)/shard_map/all_to_all | solution.py:87
  145.9 4.2 %convert_reduce_fusion = f32[192,1536]{1,0:T(8,128)S(1)} fusion(bf16[8,256,1536]{2,1,0:T(8,128)(2,1)} %bitcast.80, bf16[8,192,256]{2,1,0:T(8,128)(2,1)S(1)} %all-to-all-done.5), kind=kOutput, calls=%fused_computation | convolution fusion | flops 1214742528 | bytes 8257536 | tf_op jit(solution)/shard_map/rcd,cdf->crf/dot_general | solution.py:98
  150.2 1.1 multiply_convert_fusion.3
  151.3 0.8 pad_maximum_fusion.1
  152.2 1.5 copy.95
  153.7 23.1 %all-gather.11.cloned.1.call-done = bf16[1536,768]{1,0:T(8,128)(2,1)} async-done(((bf16[192,768]{1,0:T(8,128)(2,1)}), bf16[1536,768]{1,0:T(8,128)(2,1)}) %all-gather.11.cloned.1.call-update) | async-done | bytes 2359312 | tf_op jit(solution)/shard_map/all_gather | solution.py:115
  176.8 2.5 fusion.4
  180.1 4.6 %all-to-all-start.8 = ((f32[4,1,384]{2,1,0:T(1,128)}), f32[4,1,384]{2,1,0:T(1,128)S(1)}, u32[]{:S(2)}, u32[]{:S(2)}) async-start(f32[4,1,384]{2,1,0:T(1,128)} %reshape.102), calls=%async_computation.8 | async-start | bytes 12288 | tf_op jit(solution)/shard_map/all_to_all | solution.py:135
  184.7 32.8 %all-gather.9.cloned.1.call-done = bf16[1536,1536]{1,0:T(8,128)(2,1)} async-done(((bf16[192,1536]{1,0:T(8,128)(2,1)}), bf16[1536,1536]{1,0:T(8,128)(2,1)}) %all-gather.9.cloned.1.call-update) | async-done | bytes 4718608 | tf_op jit(solution)/shard_map/all_gather | solution.py:116
  217.5 3.8 %convolution_convert_fusion = bf16[1536,256]{1,0:T(8,128)(2,1)S(1)} fusion(bf16[1536,1536]{1,0:T(8,128)(2,1)} %all-gather.9.cloned.1.call-done, bf16[256,768]{1,0:T(8,128)(2,1)S(1)} %bitcast.88, bf16[256,768]{1,0:T(8,128)(2,1)S(1)} %bitcast.87), kind=kOutput, calls=%fused_computation.4 | convolution fusion | flops 1209925632 | bytes 6291456 | tf_op jit(solution)/shard_map/dot_general | solution.py:81
  221.3 1.0 copy.91
  222.2 4.6 %all-to-all-start.6 = ((bf16[8,4,48,256]{3,2,0,1:T(8,128)(2,1)}), bf16[8,4,48,256]{3,2,0,1:T(8,128)(2,1)S(1)}, u32[]{:S(2)}, u32[]{:S(2)}) async-start(bf16[8,4,48,256]{3,2,0,1:T(8,128)(2,1)} %copy.91), calls=%async_computation.6 | async-start | bytes 1572864 | tf_op jit(solution)/shard_map/all_to_all | solution.py:134
  227.4 3.4 %fusion.11 = bf16[1,768,256]{2,1,0:T(8,128)(2,1)} fusion(bf16[1536,768]{1,0:T(8,128)(2,1)} %all-gather.11.cloned.1.call-done, bf16[1536,256]{1,0:T(8,128)(2,1)} %bitcast.26), kind=kOutput, calls=%fused_computation.16 | convolution fusion | flops 604176384 | bytes 3538944 | tf_op jit(solution)/shard_map/dot_general | solution.py:122
  232.6 13.1 %all-reduce = f32[8,128]{1,0:T(8,128)S(1)} all-reduce(f32[8,128]{1,0:T(8,128)S(1)} %bitcast.93), channel_id=5, replica_groups=mesh['ctx'=8,'exp'=4] {'ctx'}, use_global_device_ids=true, to_apply=%region_5.6.clone | all-reduce | flops 1024 | bytes 8192
  245.8 1.2 fusion.35
  247.4 1.3 convolution_convert_fusion.3
  248.7 3.5 %all-to-all-start.7 = ((bf16[8,128,256]{2,1,0:T(8,128)(2,1)}), bf16[8,128,256]{2,1,0:T(8,128)(2,1)S(1)}, u32[]{:S(2)}, u32[]{:S(2)}) async-start(bf16[8,128,256]{2,1,0:T(8,128)(2,1)} %convolution_convert_fusion.3), calls=%async_computation.7 | async-start | bytes 1048576 | tf_op jit(solution)/shard_map/all_to_all | solution.py:145
  252.2 3.5 %fusion.12 = bf16[1,256,768]{2,1,0:T(8,128)(2,1)} fusion(bf16[1536,256]{1,0:T(8,128)(2,1)} %bitcast.31, bf16[1536,1536]{1,0:T(8,128)(2,1)} %all-gather.9.cloned.1.call-done), kind=kOutput, calls=%fused_computation.17 | convolution fusion | flops 604176384 | bytes 3538944 | tf_op jit(solution)/shard_map/dot_general | solution.py:78
  255.7 3.5 %fusion.15 = bf16[1,256,768]{2,1,0:T(8,128)(2,1)} fusion(bf16[1536,256]{1,0:T(8,128)(2,1)} %bitcast.31, bf16[1536,1536]{1,0:T(8,128)(2,1)} %all-gather.9.cloned.1.call-done), kind=kOutput, calls=%fused_computation.18 | convolution fusion | flops 604176384 | bytes 3538944 | tf_op jit(solution)/shard_map/dot_general | solution.py:75
  259.2 2.7 %all-to-all-done.7 = bf16[8,128,256]{2,1,0:T(8,128)(2,1)S(1)} async-done(((bf16[8,128,256]{2,1,0:T(8,128)(2,1)}), bf16[8,128,256]{2,1,0:T(8,128)(2,1)S(1)}, u32[]{:S(2)}, u32[]{:S(2)}) %all-to-all-start.7) | async-done | bytes 524320 | tf_op jit(solution)/shard_map/all_to_all | solution.py:145
  262.2 1.0 copy.98
  (44 shorter events, 5.9 us)
Async XLA Ops:
  7.2 23.9 %copy-start = (bf16[128,2048]{1,0:T(8,128)(2,1)S(1)}, bf16[128,2048]{1,0:T(8,128)(2,1)}, u32[]{:S(2)}) copy-start(bf16[128,2048]{1,0:T(8,128)(2,1)} %param.7) | copy-start | bytes 1572868
  7.2 126.3 %all-gather.13.cloned.1.call-start = ((), (), s32[]{:S(2)}) async-start(), calls=%async_computation.11 | async-start | bytes 3538944 | tf_op jit(solution)/shard_map/all_gather | solution.py:93
  9.2 127.3 %all-gather.15.cloned.1.call-start = ((), (), s32[]{:S(2)}) async-start(), calls=%async_computation.12 | async-start | bytes 3538944 | tf_op jit(solution)/shard_map/all_gather | solution.py:91
  10.0 126.5 %all-gather.17.cloned.1.call-start = ((), (), s32[]{:S(2)}) async-start(), calls=%async_computation.13 | async-start | bytes 3538944 | tf_op jit(solution)/shard_map/all_gather | solution.py:92
  26.2 25.5 %all-to-all-start = ((bf16[4,48,2048]{2,1,0:T(8,128)(2,1)}), bf16[4,48,2048]{2,1,0:T(8,128)(2,1)S(1)}, u32[]{:S(2)}, u32[]{:S(2)}) async-start(bf16[4,48,2048]{2,1,0:T(8,128)(2,1)} %bitcast.3), calls=%async_computation | async-start | bytes 1572864 | tf_op jit(solution)/shard_map/all_to_all | solution.py:61
  51.7 0.9 copy-start.1
  52.6 23.2 %all-to-all-start.3 = ((bf16[4,48,2048]{2,1,0:T(8,128)(2,1)}), bf16[4,48,2048]{2,1,0:T(8,128)(2,1)S(1)}, u32[]{:S(2)}, u32[]{:S(2)}) async-start(bf16[4,48,2048]{2,1,0:T(8,128)(2,1)} %bitcast.10), calls=%async_computation.3 | async-start | bytes 1572864 | tf_op jit(solution)/shard_map/all_to_all | solution.py:60
  75.8 16.9 %all-to-all-start.1 = ((bf16[8,2,24576]{2,1,0:T(2,128)(2,1)}), bf16[8,2,24576]{2,1,0:T(2,128)(2,1)}, u32[]{:S(2)}, u32[]{:S(2)}) async-start(bf16[8,2,24576]{2,1,0:T(2,128)(2,1)} %reshape.98), calls=%async_computation.1 | async-start | bytes 1572864 | tf_op jit(solution)/shard_map/all_to_all | solution.py:65
  92.7 20.3 %all-to-all-start.4 = ((bf16[8,2,24576]{2,1,0:T(2,128)(2,1)}), bf16[8,2,24576]{2,1,0:T(2,128)(2,1)S(1)}, u32[]{:S(2)}, u32[]{:S(2)}) async-start(bf16[8,2,24576]{2,1,0:T(2,128)(2,1)} %reshape.100), calls=%async_computation.4 | async-start | bytes 1572864 | tf_op jit(solution)/shard_map/all_to_all | solution.py:64
  113.0 16.8 %all-to-all-start.2 = ((bf16[8,192,256]{2,1,0:T(8,128)(2,1)}), bf16[8,192,256]{2,1,0:T(8,128)(2,1)}, u32[]{:S(2)}, u32[]{:S(2)}) async-start(bf16[8,192,256]{2,1,0:T(8,128)(2,1)} %bitcast.7), calls=%async_computation.2 | async-start | bytes 1572864 | tf_op jit(solution)/shard_map/all_to_all | solution.py:88
  129.9 16.1 %all-to-all-start.5 = ((bf16[8,192,256]{2,1,0:T(8,128)(2,1)}), bf16[8,192,256]{2,1,0:T(8,128)(2,1)S(1)}, u32[]{:S(2)}, u32[]{:S(2)}) async-start(bf16[8,192,256]{2,1,0:T(8,128)(2,1)} %bitcast.13), calls=%async_computation.5 | async-start | bytes 1572864 | tf_op jit(solution)/shard_map/all_to_all | solution.py:87
  133.4 43.4 %all-gather.11.cloned.1.call-start = ((), (), s32[]{:S(2)}) async-start(), calls=%async_computation.10 | async-start | bytes 2654208 | tf_op jit(solution)/shard_map/all_gather | solution.py:115
  150.2 26.6 %copy-start.2 = (bf16[1,768,256]{2,1,0:T(8,128)(2,1)S(1)}, bf16[1,768,256]{2,1,0:T(8,128)(2,1)}, u32[]{:S(2)}) copy-start(bf16[1,768,256]{2,1,0:T(8,128)(2,1)} %param.13) | copy-start | bytes 1179652
  151.3 66.2 %all-gather.9.cloned.1.call-start = ((), (), s32[]{:S(2)}) async-start(), calls=%async_computation.9 | async-start | bytes 5308416 | tf_op jit(solution)/shard_map/all_gather | solution.py:116
  152.2 65.3 %copy-start.3 = (bf16[1,256,768]{2,1,0:T(8,128)(2,1)S(1)}, bf16[1,256,768]{2,1,0:T(8,128)(2,1)}, u32[]{:S(2)}) copy-start(bf16[1,256,768]{2,1,0:T(8,128)(2,1)} %param.11) | copy-start | bytes 1179652
  152.2 65.3 %copy-start.4 = (bf16[1,256,768]{2,1,0:T(8,128)(2,1)S(1)}, bf16[1,256,768]{2,1,0:T(8,128)(2,1)}, u32[]{:S(2)}) copy-start(bf16[1,256,768]{2,1,0:T(8,128)(2,1)} %param.12) | copy-start | bytes 1179652
  180.1 42.1 %all-to-all-start.8 = ((f32[4,1,384]{2,1,0:T(1,128)}), f32[4,1,384]{2,1,0:T(1,128)S(1)}, u32[]{:S(2)}, u32[]{:S(2)}) async-start(f32[4,1,384]{2,1,0:T(1,128)} %reshape.102), calls=%async_computation.8 | async-start | bytes 12288 | tf_op jit(solution)/shard_map/all_to_all | solution.py:135
  221.2 5.6 %copy-start.6 = (u32[32]{0:T(128)S(1)}, u32[32]{0:T(128)}, u32[]{:S(2)}) copy-start(u32[32]{0:T(128)} %constant.31) | copy-start | bytes 388
  222.2 25.1 %all-to-all-start.6 = ((bf16[8,4,48,256]{3,2,0,1:T(8,128)(2,1)}), bf16[8,4,48,256]{3,2,0,1:T(8,128)(2,1)S(1)}, u32[]{:S(2)}, u32[]{:S(2)}) async-start(bf16[8,4,48,256]{3,2,0,1:T(8,128)(2,1)} %copy.91), calls=%async_computation.6 | async-start | bytes 1572864 | tf_op jit(solution)/shard_map/all_to_all | solution.py:134
  226.8 18.9 %copy-start.5 = (f32[128,1]{0,1:T(1,128)S(1)}, f32[128,1]{0,1:T(1,128)}, u32[]{:S(2)}) copy-start(f32[128,1]{0,1:T(1,128)} %param.10) | copy-start | bytes 1540
  248.7 13.2 %all-to-all-start.7 = ((bf16[8,128,256]{2,1,0:T(8,128)(2,1)}), bf16[8,128,256]{2,1,0:T(8,128)(2,1)S(1)}, u32[]{:S(2)}, u32[]{:S(2)}) async-start(bf16[8,128,256]{2,1,0:T(8,128)(2,1)} %convolution_convert_fusion.3), calls=%async_computation.7 | async-start | bytes 1048576 | tf_op jit(solution)/shard_map/all_to_all | solution.py:145
Sparse Core Ops, SparseCore 0:
  10.5 35.0 all-gather.12
  47.4 32.3 all-gather.14
  81.7 36.2 all-gather.16
  151.4 25.3 all-gather.10
  178.5 38.9 all-gather.8
where the time goes:
time: 271 us; the launch traced here: 270 us
  waiting for transfers between devices  121 us (45%)
  starting transfers between devices  37 us (14%)
  local copies, waits for them, and re-layouts  33.1 us (12%)
  matrix products  29.3 us (11%)
  blocking collectives  23.4 us (9%)
  between operations  14 us (5%)
  other arithmetic  12.4 us (5%)
    all_gather x1, waiting for transfers between devices, body(): lax.all_gather(grads_own, 'ctx', axis=0, tiled=True)  32.8 us
    all_gather x1, waiting for transfers between devices, body(): lax.all_gather(hidden_own, 'ctx', axis=0, tiled=True)  23.1 us
    unnamed x23, local copies, waits for them, and re-layouts  21 us
    all_to_all x1, waiting for transfers between devices, body(): lax.all_to_all(send_y, 'exp', split_axis=0, concat_axis=0, tiled=True)  19.3 us
    unnamed x1, blocking collectives  13.1 us
    all_to_all x1, waiting for transfers between devices, body(): lax.all_to_all(send_x, 'exp', split_axis=0, concat_axis=0, tiled=True)  12.9 us
    all_gather x1, blocking collectives, body(): all_ids = lax.all_gather(expert_ids, 'ctx', axis=0, tiled=True)  10.3 us
    all_to_all x1, waiting for transfers between devices, body(): lax.all_to_all(group_x, 'ctx', split_axis=2, concat_axis=0, tiled=True)  8.91 us
  transfers between devices with their start and end apart: 14, of which 10 were waited for; matrix products, arithmetic and copies ran while one was open for 24% of the time, Pallas kernels for 0%

commit v1 on v0

--- a/solution.py
+++ b/solution.py
@@ -43,7 +43,20 @@
     units = w_gate.shape[2]
     row_count = ctx_size * exp_size * capacity
     own_rows = row_count // ctx_size
-    all_ids = lax.all_gather(expert_ids, "ctx", axis=0, tiled=True)
+    world = lax.axis_size("ctx")
+    column = [(num, (num + 1) % world) for num in range(world)]
+    entries = [(num, (num - 1) % world) for num in range(world)]
+    moved, val = ([expert_ids], [expert_ids])
+    for _ in range(world // 2):
+        moved.append(lax.ppermute(moved[-1], "ctx", column))
+    ix = 0
+    while ix < (world - 1) // 2:
+        val.append(lax.ppermute(val[-1], "ctx", entries))
+        ix += 1
+    step_out = jnp.concatenate([*moved[::-1], *val[1:]], axis=0)
+    all_ids = jnp.roll(
+        step_out, shift=(lax.axis_index("ctx") - world // 2) * expert_ids.shape[0], axis=0
+    )
     tables = slot_table(all_ids.reshape(ctx_size, slot_count), expert_count, capacity)
     token_slots = jnp.repeat(tokens, route_count, axis=0)
     scaled = (

time: 271 us -> 285 us (1.052)
  waiting for transfers between devices: 121 us -> 133 us
  starting transfers between devices: 37 us -> 47.5 us
  blocking collectives: 23.4 us -> 13.1 us
    all_gather x1 -> x0, blocking collectives: 10.3 us -> none  [body(): all_ids = lax.all_gather(expert_ids, 'ctx', axis=0, tiled=True)]
    ppermute x0 -> x7, starting transfers between devices: none -> 8.71 us  [the longest x3 8.19 us: body(): val.append(lax.ppermute(val[-1], 'ctx', entries))]
    ppermute x0 -> x7, waiting for transfers between devices: none -> 7.61 us  [the longest x4 7.53 us: body(): moved.append(lax.ppermute(moved[-1], 'ctx', column))]
    all_to_all x1, waiting for transfers between devices: 7.3 us -> 11.5 us  [body(): lax.all_to_all(group_y, 'ctx', split_axis=2, concat_axis=0, tiled=True)]
    unnamed x23 -> x38, local copies, waits for them, and re-layouts: 21 us -> 22.4 us
  transfers between devices with their start and end apart: 14 -> 21, of which waited for: 10 -> 15; matrix products, arithmetic and copies ran while one was open for 24% -> 23% of each run, Pallas kernels for 0% -> 0%
where the time goes in v1:
time: 285 us; the launch traced here: 284 us
  waiting for transfers between devices  133 us (47%)
  starting transfers between devices  47.5 us (17%)
  local copies, waits for them, and re-layouts  34.5 us (12%)
  matrix products  29.3 us (10%)
  between operations  14 us (5%)
  blocking collectives  13.1 us (5%)
  other arithmetic  12.4 us (4%)
    all_gather x1, waiting for transfers between devices, body(): lax.all_gather(grads_own, 'ctx', axis=0, tiled=True)  32.8 us
    all_gather x1, waiting for transfers between devices, body(): lax.all_gather(hidden_own, 'ctx', axis=0, tiled=True)  25.3 us
    unnamed x38, local copies, waits for them, and re-layouts  22.4 us
    all_to_all x1, waiting for transfers between devices, body(): lax.all_to_all(send_y, 'exp', split_axis=0, concat_axis=0, tiled=True)  16.7 us
    unnamed x1, blocking collectives  13.1 us
    all_to_all x1, waiting for transfers between devices, body(): lax.all_to_all(send_x, 'exp', split_axis=0, concat_axis=0, tiled=True)  12.3 us
    all_to_all x1, waiting for transfers between devices, body(): lax.all_to_all(group_y, 'ctx', split_axis=2, concat_axis=0, tiled=True)  11.5 us
    all_to_all x1, waiting for transfers between devices, body(): lax.all_to_all(group_x, 'ctx', split_axis=2, concat_axis=0, tiled=True)  11.3 us
  transfers between devices with their start and end apart: 21, of which 15 were waited for; matrix products, arithmetic and copies ran while one was open for 23% of the time, Pallas kernels for 0%

profile of v1, /device:TPU:0, one launch (start us, length us, event | category | flops | bytes accessed | tf_op | source)
XLA Modules:
  0.0 283.8 jit_solution(12998682724322358080)
XLA Ops:
  7.2 2.0 copy.89
  10.5 2.9 %collective-permute-start.4 = (s32[128,1]{0,1:T(1,128)}, s32[128,1]{0,1:T(1,128)S(1)}, u32[]{:S(2)}, u32[]{:S(2)}) collective-permute-start(s32[128,1]{0,1:T(1,128)} %param.9), channel_id=1, source_target_pairs={{0,28},{4,0},{8,4},{12,8},{16,12},{20,16},{24,20},{28,24},{1,29},{... | collective-permute-start | bytes 1544 | tf_op jit(solution)/shard_map/ppermute | solution.py:54
  13.5 1.3 collective-permute-done
  14.8 3.9 %collective-permute-done.1 = s32[128,1]{0,1:T(1,128)S(1)} collective-permute-done((s32[128,1]{0,1:T(1,128)S(1)}, s32[128,1]{0,1:T(1,128)S(1)}, u32[]{:S(2)}, u32[]{:S(2)}) %collective-permute-start.1) | collective-permute-done | bytes 544 | tf_op jit(solution)/shard_map/ppermute | solution.py:51
  18.6 2.6 collective-permute-start.5
  21.3 1.2 collective-permute-done.2
  22.6 2.6 collective-permute-start.6
  25.2 1.2 collective-permute-done.3
  27.9 2.5 select_reduce_fusion
  30.6 2.4 convolution_convert_fusion.2
  33.0 5.6 %all-to-all-start = ((bf16[4,48,2048]{2,1,0:T(8,128)(2,1)}), bf16[4,48,2048]{2,1,0:T(8,128)(2,1)S(1)}, u32[]{:S(2)}, u32[]{:S(2)}) async-start(bf16[4,48,2048]{2,1,0:T(8,128)(2,1)} %bitcast.3), calls=%async_computation | async-start | bytes 1572864 | tf_op jit(solution)/shard_map/all_to_all | solution.py:74
  38.6 1.3 convolution_convert_fusion.1
  39.9 16.7 %all-to-all-done = bf16[4,48,2048]{2,1,0:T(8,128)(2,1)S(1)} async-done(((bf16[4,48,2048]{2,1,0:T(8,128)(2,1)}), bf16[4,48,2048]{2,1,0:T(8,128)(2,1)S(1)}, u32[]{:S(2)}, u32[]{:S(2)}) %all-to-all-start) | async-done | bytes 786464 | tf_op jit(solution)/shard_map/all_to_all | solution.py:74
  57.5 3.5 %all-to-all-start.3 = ((bf16[4,48,2048]{2,1,0:T(8,128)(2,1)}), bf16[4,48,2048]{2,1,0:T(8,128)(2,1)S(1)}, u32[]{:S(2)}, u32[]{:S(2)}) async-start(bf16[4,48,2048]{2,1,0:T(8,128)(2,1)} %bitcast.10), calls=%async_computation.3 | async-start | bytes 1572864 | tf_op jit(solution)/shard_map/all_to_all | solution.py:73
  61.0 2.9 %copy.86 = bf16[4,48,2048]{1,0,2:T(4,128)(2,1)S(1)} copy(bf16[4,48,2048]{2,1,0:T(8,128)(2,1)} %copy-done.1) | data formatting | bytes 1572864 | tf_op jit(solution)/shard_map/all_to_all | solution.py:74
  63.9 4.0 %reshape.98 = bf16[8,2,24576]{2,1,0:T(2,128)(2,1)} reshape(bf16[2048,4,48]{2,1,0:T(4,128)(2,1)S(1)} %bitcast.76) | data formatting | bytes 1572864
  67.8 12.3 %all-to-all-done.3 = bf16[4,48,2048]{2,1,0:T(8,128)(2,1)S(1)} async-done(((bf16[4,48,2048]{2,1,0:T(8,128)(2,1)}), bf16[4,48,2048]{2,1,0:T(8,128)(2,1)S(1)}, u32[]{:S(2)}, u32[]{:S(2)}) %all-to-all-start.3) | async-done | bytes 786464 | tf_op jit(solution)/shard_map/all_to_all | solution.py:73
  80.1 5.3 %all-to-all-start.1 = ((bf16[8,2,24576]{2,1,0:T(2,128)(2,1)}), bf16[8,2,24576]{2,1,0:T(2,128)(2,1)}, u32[]{:S(2)}, u32[]{:S(2)}) async-start(bf16[8,2,24576]{2,1,0:T(2,128)(2,1)} %reshape.98), calls=%async_computation.1 | async-start | bytes 1572864 | tf_op jit(solution)/shard_map/all_to_all | solution.py:78
  85.4 1.4 copy.91
  86.7 4.0 %reshape.100 = bf16[8,2,24576]{2,1,0:T(2,128)(2,1)} reshape(bf16[2048,4,48]{2,1,0:T(4,128)(2,1)S(1)} %bitcast.77) | data formatting | bytes 1572864
  90.7 11.5 %all-to-all-done.1 = bf16[8,2,24576]{2,1,0:T(2,128)(2,1)} async-done(((bf16[8,2,24576]{2,1,0:T(2,128)(2,1)}), bf16[8,2,24576]{2,1,0:T(2,128)(2,1)}, u32[]{:S(2)}, u32[]{:S(2)}) %all-to-all-start.1) | async-done | bytes 786464 | tf_op jit(solution)/shard_map/all_to_all | solution.py:78
  102.2 3.5 %all-to-all-start.4 = ((bf16[8,2,24576]{2,1,0:T(2,128)(2,1)}), bf16[8,2,24576]{2,1,0:T(2,128)(2,1)S(1)}, u32[]{:S(2)}, u32[]{:S(2)}) async-start(bf16[8,2,24576]{2,1,0:T(2,128)(2,1)} %reshape.100), calls=%async_computation.4 | async-start | bytes 1572864 | tf_op jit(solution)/shard_map/all_to_all | solution.py:77
  105.8 5.7 %reshape.99 = bf16[2048,4,48]{2,1,0:T(4,128)(2,1)S(1)} reshape(bf16[8,2,24576]{2,1,0:T(2,128)(2,1)} %all-to-all-done.1) | data formatting | bytes 1572864
  111.5 2.1 copy.105
  113.6 11.3 %all-to-all-done.4 = bf16[8,2,24576]{2,1,0:T(2,128)(2,1)S(1)} async-done(((bf16[8,2,24576]{2,1,0:T(2,128)(2,1)}), bf16[8,2,24576]{2,1,0:T(2,128)(2,1)S(1)}, u32[]{:S(2)}, u32[]{:S(2)}) %all-to-all-start.4) | async-done | bytes 786464 | tf_op jit(solution)/shard_map/all_to_all | solution.py:77
  124.9 4.4 %all-to-all-start.2 = ((bf16[8,192,256]{2,1,0:T(8,128)(2,1)}), bf16[8,192,256]{2,1,0:T(8,128)(2,1)}, u32[]{:S(2)}, u32[]{:S(2)}) async-start(bf16[8,192,256]{2,1,0:T(8,128)(2,1)} %bitcast.7), calls=%async_computation.2 | async-start | bytes 1572864 | tf_op jit(solution)/shard_map/all_to_all | solution.py:101
  129.3 2.1 reshape.101
  131.4 2.1 copy.92
  133.5 8.2 %all-to-all-done.2 = bf16[8,192,256]{2,1,0:T(8,128)(2,1)} async-done(((bf16[8,192,256]{2,1,0:T(8,128)(2,1)}), bf16[8,192,256]{2,1,0:T(8,128)(2,1)}, u32[]{:S(2)}, u32[]{:S(2)}) %all-to-all-start.2) | async-done | bytes 786464 | tf_op jit(solution)/shard_map/all_to_all | solution.py:101
  141.7 3.5 %all-to-all-start.5 = ((bf16[8,192,256]{2,1,0:T(8,128)(2,1)}), bf16[8,192,256]{2,1,0:T(8,128)(2,1)S(1)}, u32[]{:S(2)}, u32[]{:S(2)}) async-start(bf16[8,192,256]{2,1,0:T(8,128)(2,1)} %bitcast.13), calls=%async_computation.5 | async-start | bytes 1572864 | tf_op jit(solution)/shard_map/all_to_all | solution.py:100
  145.3 3.0 %convert_reduce_fusion.1 = f32[192,768]{1,0:T(8,128)S(1)} fusion(bf16[768,8,256]{0,2,1:T(8,128)(2,1)} %bitcast.95, bf16[8,192,256]{2,1,0:T(8,128)(2,1)} %all-to-all-done.2), kind=kOutput, calls=%fused_computation.2 | convolution fusion | flops 607371264 | bytes 4521984 | tf_op jit(solution)/shard_map/rcd,fcd->crf/dot_general | solution.py:119
  148.3 5.9 %pad_maximum_fusion = bf16[2048,1536]{1,0:T(8,128)(2,1)} fusion(bf16[2048,768]{1,0:T(8,128)(2,1)} %bitcast.83, bf16[2048,768]{1,0:T(8,128)(2,1)} %bitcast.82), kind=kLoop, calls=%fused_computation.1 | loop fusion | flops 12582912 | bytes 12582912 | tf_op jit(solution)/shard_map/concatenate | solution.py:108
  154.3 3.5 %all-to-all-done.5 = bf16[8,192,256]{2,1,0:T(8,128)(2,1)S(1)} async-done(((bf16[8,192,256]{2,1,0:T(8,128)(2,1)}), bf16[8,192,256]{2,1,0:T(8,128)(2,1)S(1)}, u32[]{:S(2)}, u32[]{:S(2)}) %all-to-all-start.5) | async-done | bytes 786464 | tf_op jit(solution)/shard_map/all_to_all | solution.py:100
  157.8 4.2 %convert_reduce_fusion = f32[192,1536]{1,0:T(8,128)S(1)} fusion(bf16[8,256,1536]{2,1,0:T(8,128)(2,1)} %bitcast.80, bf16[8,192,256]{2,1,0:T(8,128)(2,1)S(1)} %all-to-all-done.5), kind=kOutput, calls=%fused_computation | convolution fusion | flops 1214742528 | bytes 8257536 | tf_op jit(solution)/shard_map/rcd,cdf->crf/dot_general | solution.py:111
  164.1 1.5 copy.97
  165.5 25.3 %all-gather.11.cloned.1.call-done = bf16[1536,768]{1,0:T(8,128)(2,1)} async-done(((bf16[192,768]{1,0:T(8,128)(2,1)}), bf16[1536,768]{1,0:T(8,128)(2,1)}) %all-gather.11.cloned.1.call-update) | async-done | bytes 2359312 | tf_op jit(solution)/shard_map/all_gather | solution.py:128
  190.9 2.5 fusion.4
  194.1 4.6 %all-to-all-start.8 = ((f32[4,1,384]{2,1,0:T(1,128)}), f32[4,1,384]{2,1,0:T(1,128)S(1)}, u32[]{:S(2)}, u32[]{:S(2)}) async-start(f32[4,1,384]{2,1,0:T(1,128)} %reshape.102), calls=%async_computation.8 | async-start | bytes 12288 | tf_op jit(solution)/shard_map/all_to_all | solution.py:148
  198.7 32.8 %all-gather.9.cloned.1.call-done = bf16[1536,1536]{1,0:T(8,128)(2,1)} async-done(((bf16[192,1536]{1,0:T(8,128)(2,1)}), bf16[1536,1536]{1,0:T(8,128)(2,1)}) %all-gather.9.cloned.1.call-update) | async-done | bytes 4718608 | tf_op jit(solution)/shard_map/all_gather | solution.py:129
  231.6 3.8 %convolution_convert_fusion = bf16[1536,256]{1,0:T(8,128)(2,1)S(1)} fusion(bf16[1536,1536]{1,0:T(8,128)(2,1)} %all-gather.9.cloned.1.call-done, bf16[256,768]{1,0:T(8,128)(2,1)S(1)} %bitcast.88, bf16[256,768]{1,0:T(8,128)(2,1)S(1)} %bitcast.87), kind=kOutput, calls=%fused_computation.4 | convolution fusion | flops 1209925632 | bytes 6291456 | tf_op jit(solution)/shard_map/dot_general | solution.py:94
  236.3 4.6 %all-to-all-start.6 = ((bf16[8,4,48,256]{3,2,0,1:T(8,128)(2,1)}), bf16[8,4,48,256]{3,2,0,1:T(8,128)(2,1)S(1)}, u32[]{:S(2)}, u32[]{:S(2)}) async-start(bf16[8,4,48,256]{3,2,0,1:T(8,128)(2,1)} %copy.93), calls=%async_computation.6 | async-start | bytes 1572864 | tf_op jit(solution)/shard_map/all_to_all | solution.py:147
  241.5 3.4 %fusion.11 = bf16[1,768,256]{2,1,0:T(8,128)(2,1)} fusion(bf16[1536,768]{1,0:T(8,128)(2,1)} %all-gather.11.cloned.1.call-done, bf16[1536,256]{1,0:T(8,128)(2,1)} %bitcast.26), kind=kOutput, calls=%fused_computation.16 | convolution fusion | flops 604176384 | bytes 3538944 | tf_op jit(solution)/shard_map/dot_general | solution.py:135
  246.7 13.1 %all-reduce = f32[8,128]{1,0:T(8,128)S(1)} all-reduce(f32[8,128]{1,0:T(8,128)S(1)} %bitcast.93), channel_id=5, replica_groups=mesh['ctx'=8,'exp'=4] {'ctx'}, use_global_device_ids=true, to_apply=%region_5.6.clone | all-reduce | flops 1024 | bytes 8192
  261.5 1.3 convolution_convert_fusion.3
  262.8 3.5 %all-to-all-start.7 = ((bf16[8,128,256]{2,1,0:T(8,128)(2,1)}), bf16[8,128,256]{2,1,0:T(8,128)(2,1)S(1)}, u32[]{:S(2)}, u32[]{:S(2)}) async-start(bf16[8,128,256]{2,1,0:T(8,128)(2,1)} %convolution_convert_fusion.3), calls=%async_computation.7 | async-start | bytes 1048576 | tf_op jit(solution)/shard_map/all_to_all | solution.py:158
  266.3 3.5 %fusion.12 = bf16[1,256,768]{2,1,0:T(8,128)(2,1)} fusion(bf16[1536,256]{1,0:T(8,128)(2,1)} %bitcast.31, bf16[1536,1536]{1,0:T(8,128)(2,1)} %all-gather.9.cloned.1.call-done), kind=kOutput, calls=%fused_computation.17 | convolution fusion | flops 604176384 | bytes 3538944 | tf_op jit(solution)/shard_map/dot_general | solution.py:91
  269.8 3.5 %fusion.15 = bf16[1,256,768]{2,1,0:T(8,128)(2,1)} fusion(bf16[1536,256]{1,0:T(8,128)(2,1)} %bitcast.31, bf16[1536,1536]{1,0:T(8,128)(2,1)} %all-gather.9.cloned.1.call-done), kind=kOutput, calls=%fused_computation.18 | convolution fusion | flops 604176384 | bytes 3538944 | tf_op jit(solution)/shard_map/dot_general | solution.py:88
  273.3 2.7 all-to-all-done.7
  (74 shorter events, 13.2 us)
Async XLA Ops:
  7.2 31.5 %copy-start = (bf16[128,2048]{1,0:T(8,128)(2,1)S(1)}, bf16[128,2048]{1,0:T(8,128)(2,1)}, u32[]{:S(2)}) copy-start(bf16[128,2048]{1,0:T(8,128)(2,1)} %param.7) | copy-start | bytes 1572868
  7.2 138.1 %all-gather.13.cloned.1.call-start = ((), (), s32[]{:S(2)}) async-start(), calls=%async_computation.11 | async-start | bytes 3538944 | tf_op jit(solution)/shard_map/all_gather | solution.py:106
  9.2 139.1 %all-gather.15.cloned.1.call-start = ((), (), s32[]{:S(2)}) async-start(), calls=%async_computation.12 | async-start | bytes 3538944 | tf_op jit(solution)/shard_map/all_gather | solution.py:104
  10.0 138.4 %all-gather.17.cloned.1.call-start = ((), (), s32[]{:S(2)}) async-start(), calls=%async_computation.13 | async-start | bytes 3538944 | tf_op jit(solution)/shard_map/all_gather | solution.py:105
  10.0 4.7 %collective-permute-start = (s32[128,1]{0,1:T(1,128)}, s32[128,1]{0,1:T(1,128)S(1)}, u32[]{:S(2)}, u32[]{:S(2)}) collective-permute-start(s32[128,1]{0,1:T(1,128)} %param.9), channel_id=1, source_target_pairs={{0,4},{4,8},{8,12},{12,16},{16,20},{20,24},{24,28},{28,0},{1,5},{5... | collective-permute-start | bytes 1544 | tf_op jit(solution)/shard_map/ppermute | solution.py:51
  10.5 8.1 %collective-permute-start.4 = (s32[128,1]{0,1:T(1,128)}, s32[128,1]{0,1:T(1,128)S(1)}, u32[]{:S(2)}, u32[]{:S(2)}) collective-permute-start(s32[128,1]{0,1:T(1,128)} %param.9), channel_id=1, source_target_pairs={{0,28},{4,0},{8,4},{12,8},{16,12},{20,16},{24,20},{28,24},{1,29},{... | collective-permute-start | bytes 1544 | tf_op jit(solution)/shard_map/ppermute | solution.py:54
  14.8 3.9 %collective-permute-start.1 = (s32[128,1]{0,1:T(1,128)S(1)}, s32[128,1]{0,1:T(1,128)S(1)}, u32[]{:S(2)}, u32[]{:S(2)}) collective-permute-start(s32[128,1]{0,1:T(1,128)S(1)} %collective-permute-done), channel_id=1, source_target_pairs={{0,4},{4,8},{8,12},{12,16},{16,20},{20,24},{24,28},{28,0},{1,5},{5... | collective-permute-start | bytes 1544 | tf_op jit(solution)/shard_map/ppermute | solution.py:51
  18.6 3.9 %collective-permute-start.2 = (s32[128,1]{0,1:T(1,128)S(1)}, s32[128,1]{0,1:T(1,128)S(1)}, u32[]{:S(2)}, u32[]{:S(2)}) collective-permute-start(s32[128,1]{0,1:T(1,128)S(1)} %collective-permute-done.1), channel_id=1, source_target_pairs={{0,4},{4,8},{8,12},{12,16},{16,20},{20,24},{24,28},{28,0},{1,5},{5... | collective-permute-start | bytes 1544 | tf_op jit(solution)/shard_map/ppermute | solution.py:51
  18.6 3.9 %collective-permute-start.5 = (s32[128,1]{0,1:T(1,128)S(1)}, s32[128,1]{0,1:T(1,128)S(1)}, u32[]{:S(2)}, u32[]{:S(2)}) collective-permute-start(s32[128,1]{0,1:T(1,128)S(1)} %collective-permute-done.4), channel_id=1, source_target_pairs={{0,28},{4,0},{8,4},{12,8},{16,12},{20,16},{24,20},{28,24},{1,29},{... | collective-permute-start | bytes 1544 | tf_op jit(solution)/shard_map/ppermute | solution.py:54
  22.5 3.9 %collective-permute-start.3 = (s32[128,1]{0,1:T(1,128)S(1)}, s32[128,1]{0,1:T(1,128)S(1)}, u32[]{:S(2)}, u32[]{:S(2)}) collective-permute-start(s32[128,1]{0,1:T(1,128)S(1)} %collective-permute-done.2), channel_id=1, source_target_pairs={{0,4},{4,8},{8,12},{12,16},{16,20},{20,24},{24,28},{28,0},{1,5},{5... | collective-permute-start | bytes 1544 | tf_op jit(solution)/shard_map/ppermute | solution.py:51
  22.6 4.5 %collective-permute-start.6 = (s32[128,1]{0,1:T(1,128)S(1)}, s32[128,1]{0,1:T(1,128)S(1)}, u32[]{:S(2)}, u32[]{:S(2)}) collective-permute-start(s32[128,1]{0,1:T(1,128)S(1)} %collective-permute-done.5), channel_id=1, source_target_pairs={{0,28},{4,0},{8,4},{12,8},{16,12},{20,16},{24,20},{28,24},{1,29},{... | collective-permute-start | bytes 1544 | tf_op jit(solution)/shard_map/ppermute | solution.py:54
  33.0 23.6 %all-to-all-start = ((bf16[4,48,2048]{2,1,0:T(8,128)(2,1)}), bf16[4,48,2048]{2,1,0:T(8,128)(2,1)S(1)}, u32[]{:S(2)}, u32[]{:S(2)}) async-start(bf16[4,48,2048]{2,1,0:T(8,128)(2,1)} %bitcast.3), calls=%async_computation | async-start | bytes 1572864 | tf_op jit(solution)/shard_map/all_to_all | solution.py:74
  56.6 0.9 copy-start.1
  57.5 22.6 %all-to-all-start.3 = ((bf16[4,48,2048]{2,1,0:T(8,128)(2,1)}), bf16[4,48,2048]{2,1,0:T(8,128)(2,1)S(1)}, u32[]{:S(2)}, u32[]{:S(2)}) async-start(bf16[4,48,2048]{2,1,0:T(8,128)(2,1)} %bitcast.10), calls=%async_computation.3 | async-start | bytes 1572864 | tf_op jit(solution)/shard_map/all_to_all | solution.py:73
  80.1 22.1 %all-to-all-start.1 = ((bf16[8,2,24576]{2,1,0:T(2,128)(2,1)}), bf16[8,2,24576]{2,1,0:T(2,128)(2,1)}, u32[]{:S(2)}, u32[]{:S(2)}) async-start(bf16[8,2,24576]{2,1,0:T(2,128)(2,1)} %reshape.98), calls=%async_computation.1 | async-start | bytes 1572864 | tf_op jit(solution)/shard_map/all_to_all | solution.py:78
  102.2 22.6 %all-to-all-start.4 = ((bf16[8,2,24576]{2,1,0:T(2,128)(2,1)}), bf16[8,2,24576]{2,1,0:T(2,128)(2,1)S(1)}, u32[]{:S(2)}, u32[]{:S(2)}) async-start(bf16[8,2,24576]{2,1,0:T(2,128)(2,1)} %reshape.100), calls=%async_computation.4 | async-start | bytes 1572864 | tf_op jit(solution)/shard_map/all_to_all | solution.py:77
  124.9 16.8 %all-to-all-start.2 = ((bf16[8,192,256]{2,1,0:T(8,128)(2,1)}), bf16[8,192,256]{2,1,0:T(8,128)(2,1)}, u32[]{:S(2)}, u32[]{:S(2)}) async-start(bf16[8,192,256]{2,1,0:T(8,128)(2,1)} %bitcast.7), calls=%async_computation.2 | async-start | bytes 1572864 | tf_op jit(solution)/shard_map/all_to_all | solution.py:101
  141.7 16.1 %all-to-all-start.5 = ((bf16[8,192,256]{2,1,0:T(8,128)(2,1)}), bf16[8,192,256]{2,1,0:T(8,128)(2,1)S(1)}, u32[]{:S(2)}, u32[]{:S(2)}) async-start(bf16[8,192,256]{2,1,0:T(8,128)(2,1)} %bitcast.13), calls=%async_computation.5 | async-start | bytes 1572864 | tf_op jit(solution)/shard_map/all_to_all | solution.py:100
  145.2 45.6 %all-gather.11.cloned.1.call-start = ((), (), s32[]{:S(2)}) async-start(), calls=%async_computation.10 | async-start | bytes 2654208 | tf_op jit(solution)/shard_map/all_gather | solution.py:128
  162.0 28.8 %copy-start.2 = (bf16[1,768,256]{2,1,0:T(8,128)(2,1)S(1)}, bf16[1,768,256]{2,1,0:T(8,128)(2,1)}, u32[]{:S(2)}) copy-start(bf16[1,768,256]{2,1,0:T(8,128)(2,1)} %param.13) | copy-start | bytes 1179652
  163.1 68.4 %all-gather.9.cloned.1.call-start = ((), (), s32[]{:S(2)}) async-start(), calls=%async_computation.9 | async-start | bytes 5308416 | tf_op jit(solution)/shard_map/all_gather | solution.py:129
  164.0 67.5 %copy-start.3 = (bf16[1,256,768]{2,1,0:T(8,128)(2,1)S(1)}, bf16[1,256,768]{2,1,0:T(8,128)(2,1)}, u32[]{:S(2)}) copy-start(bf16[1,256,768]{2,1,0:T(8,128)(2,1)} %param.11) | copy-start | bytes 1179652
  164.0 67.5 %copy-start.4 = (bf16[1,256,768]{2,1,0:T(8,128)(2,1)S(1)}, bf16[1,256,768]{2,1,0:T(8,128)(2,1)}, u32[]{:S(2)}) copy-start(bf16[1,256,768]{2,1,0:T(8,128)(2,1)} %param.12) | copy-start | bytes 1179652
  194.1 42.1 %all-to-all-start.8 = ((f32[4,1,384]{2,1,0:T(1,128)}), f32[4,1,384]{2,1,0:T(1,128)S(1)}, u32[]{:S(2)}, u32[]{:S(2)}) async-start(f32[4,1,384]{2,1,0:T(1,128)} %reshape.102), calls=%async_computation.8 | async-start | bytes 12288 | tf_op jit(solution)/shard_map/all_to_all | solution.py:148
  235.3 5.6 %copy-start.6 = (u32[32]{0:T(128)S(1)}, u32[32]{0:T(128)}, u32[]{:S(2)}) copy-start(u32[32]{0:T(128)} %constant.57) | copy-start | bytes 388
  236.3 25.1 %all-to-all-start.6 = ((bf16[8,4,48,256]{3,2,0,1:T(8,128)(2,1)}), bf16[8,4,48,256]{3,2,0,1:T(8,128)(2,1)S(1)}, u32[]{:S(2)}, u32[]{:S(2)}) async-start(bf16[8,4,48,256]{3,2,0,1:T(8,128)(2,1)} %copy.93), calls=%async_computation.6 | async-start | bytes 1572864 | tf_op jit(solution)/shard_map/all_to_all | solution.py:147
  240.9 18.9 %copy-start.5 = (f32[128,1]{0,1:T(1,128)S(1)}, f32[128,1]{0,1:T(1,128)}, u32[]{:S(2)}) copy-start(f32[128,1]{0,1:T(1,128)} %param.10) | copy-start | bytes 1540
  262.8 13.2 %all-to-all-start.7 = ((bf16[8,128,256]{2,1,0:T(8,128)(2,1)}), bf16[8,128,256]{2,1,0:T(8,128)(2,1)S(1)}, u32[]{:S(2)}, u32[]{:S(2)}) async-start(bf16[8,128,256]{2,1,0:T(8,128)(2,1)} %convolution_convert_fusion.3), calls=%async_computation.7 | async-start | bytes 1048576 | tf_op jit(solution)/shard_map/all_to_all | solution.py:158
Sparse Core Ops, SparseCore 0:
  10.5 35.0 all-gather.12
  47.4 32.3 all-gather.14
  81.7 42.0 all-gather.16
  163.2 27.5 all-gather.10
  192.6 38.9 all-gather.8
